TPU v7x, 32 devices: a whole 2x2x4 slice. The times are simulated.
32 devices in a mesh: outer: 4 (over y, core), row: 4 (over z), col: 2 (over x).
Axes of the slice: x: 2, y: 2, z: 4, core: 2. Of those that a mesh axis runs over, the one named last changes fastest.
Arguments:
- activations: bfloat16 [2048, 9216], P(('outer', 'col'), 'row'), may hold values from -13 to 13
- out_grads: bfloat16 [2048, 8192], P(('outer', 'row'), 'col'), may hold values from -13 to 13
- row_moment: float32 [9216], P(('row', 'outer')), may hold values from 0.3 to 3
- col_moment: float32 [8192], P('col'), may hold values from 0.3 to 3
Outputs:
- update: bfloat16 [9216, 8192], P(('row', 'outer'), 'col')
- new_row: float32 [9216], P(('row', 'outer'))
- new_col: float32 [8192], P('col')
All inputs are finite; a program needn't handle non-finite values.
Results may differ from a plain program's by a relative error of at most 0.001.
Values may be sent and summed in bfloat16 or wider, within the bound.
A program may use at most 128 MiB of HBM per device.

v0:
```python
import jax
import jax.numpy as jnp
from jax import lax
from jax.sharding import PartitionSpec as P

D = 9216
F = 8192
STEP = 2


def body(activations, out_grads, row_moment, col_moment):
    row_count = row_moment.shape[0]
    quarter = lax.axis_index("outer") * row_count
    token_count = activations.shape[0] * lax.axis_size("col") * lax.axis_size("outer")
    contract = (((0,), (0,)), ((), ()))
    grads_all = lax.all_gather(out_grads, ("outer", "row"), axis=0, tiled=True)
    columns = lax.dynamic_slice_in_dim(
        lax.all_gather(activations, ("outer", "col"), axis=0, tiled=True), quarter, row_count, 1
    )
    gradient = lax.dot_general(columns, grads_all, contract, preferred_element_type=jnp.float32)
    gradient = gradient * (1.0 / token_count**0.5)
    squares = gradient * gradient
    col_squares, old_total = lax.psum(
        (jnp.sum(squares, axis=0), jnp.sum(row_moment)), ("outer", "row")
    )
    row_squares, grad_total = lax.psum((jnp.sum(squares, axis=1), jnp.sum(col_squares)), "col")
    decay_rate = 1.0 - STEP ** (-0.8)
    new_row = decay_rate * row_moment + (1.0 - decay_rate) * row_squares / F
    new_col = decay_rate * col_moment + (1.0 - decay_rate) * col_squares / D
    moment_total = decay_rate * old_total + (1.0 - decay_rate) * grad_total / F
    factor = lax.rsqrt(new_row[:, None] * new_col[None, :] * (D / moment_total))
    update = (gradient * factor).astype(jnp.bfloat16)
    return (update, new_row, new_col)


def solution(mesh):
    return jax.shard_map(
        body,
        mesh=mesh,
        in_specs=(
            P(("outer", "col"), "row"),
            P(("outer", "row"), "col"),
            P(("row", "outer")),
            P("col"),
        ),
        out_specs=(P(("row", "outer"), "col"), P(("row", "outer")), P("col")),
        check_vma=False,
    )
```

profile of v0, /device:TPU:0, one launch (start us, length us, event | category | flops | bytes accessed | tf_op | source)
XLA Modules:
  0.0 298.9 jit_solution(16557002799071541110)
XLA Ops:
  7.2 0.0 all-gather.3.cloned.1.call-start
  7.2 0.7 all-gather.3.cloned.1.call-update
  7.9 0.0 all-gather.5.cloned.1.call-start
  7.9 0.7 all-gather.5.cloned.1.call-update
  8.7 1.3 reduce_sum.38
  9.9 0.0 copy-start.1
  9.9 0.0 copy-start.2
  10.0 61.4 %all-gather.3.cloned.1.call-done = bf16[2048,2304]{1,0:T(8,128)(2,1)} async-done(((bf16[256,2304]{1,0:T(8,128)(2,1)}), bf16[2048,2304]{1,0:T(8,128)(2,1)}) %all-gather.3.cloned.1.call-update) | async-done | bytes 9437200 | tf_op jit(solution)/shard_map/all_gather | solution.py:18
  71.3 128.7 %all-gather.5.cloned.1.call-done = bf16[2048,4096]{1,0:T(8,128)(2,1)} async-done(((bf16[128,4096]{1,0:T(8,128)(2,1)}), bf16[2048,4096]{1,0:T(8,128)(2,1)}) %all-gather.5.cloned.1.call-update) | async-done | bytes 16777232 | tf_op jit(solution)/shard_map/all_gather | solution.py:16
  200.0 17.7 %multiply_reduce_fusion.1 = (f32[576]{0:T(1024)S(1)}, f32[4096]{0:T(1024)S(1)}, f32[576,4096]{1,0:T(8,128)}) fusion(bf16[2048,4096]{1,0:T(8,128)(2,1)} %all-gather.5.cloned.1.call-done, bf16[2048,2304]{1,0:T(8,128)(2,1)} %all-gather.3.cloned.1.call-done, s32[]{:T(128)S(6)} %select_n.3), kind=kOutput, calls=%fused_computation.2 | convolution fusion | flops 9673108480 | bytes 28854532 | tf_op jit(solution)/shard_map/dot_general | solution.py:20
  217.7 58.9 %all-reduce = (f32[]{:T(128)}, f32[4096]{0:T(1024)S(1)}) all-reduce(f32[]{:T(128)} %reduce_sum.38, f32[4096]{0:T(1024)S(1)} %get-tuple-element.4), channel_id=1, replica_groups=mesh['outer'=4,'row'=4,'col'=2] {'outer','row'}, use_global_device_ids=true, to_apply=%region_5.0 | all-reduce | flops 4097 | bytes 32776 | tf_op jit(solution)/shard_map/psum | solution.py:23
  276.6 0.0 copy-done.1
  276.6 0.6 multiply_add_fusion
  277.2 0.0 copy-start
  277.2 5.7 %all-reduce.1 = (f32[]{:T(128)}, f32[576]{0:T(1024)S(1)}) all-reduce(f32[]{:T(128)} %get-tuple-element.10, f32[576]{0:T(1024)S(1)} %get-tuple-element.3), channel_id=1, replica_groups=mesh['outer'=4,'row'=4,'col'=2] {'col'}, use_global_device_ids=true, to_apply=%region_7.0 | all-reduce | flops 577 | bytes 4616 | tf_op jit(solution)/shard_map/psum | solution.py:26
  282.9 0.0 copy-done.2
  282.9 0.0 copy-start.3
  284.3 7.8 %multiply_convert_fusion = bf16[576,4096]{1,0:T(8,128)(2,1)} fusion(f32[576,4096]{1,0:T(8,128)} %get-tuple-element.11, f32[]{:T(128)S(6)} %div.23, f32[4096]{0:T(1024)S(1)} %get-tuple-element.9, f32[576]{0:T(1024)S(1)} %multiply_add_fusion.1), kind=kLoop, calls=%fused_computation | loop fusion | flops 11796480 | bytes 14174468 | tf_op jit(solution)/shard_map/convert_element_type | solution.py:32
  292.0 0.0 copy-done
  292.0 0.0 copy-done.3
  (1 shorter events, 0.0 us)
Async XLA Ops:
  7.2 64.1 %all-gather.3.cloned.1.call-start = ((), (), s32[]{:S(2)}) async-start(), calls=%async_computation | async-start | bytes 10616832 | tf_op jit(solution)/shard_map/all_gather | solution.py:18
  7.9 192.1 %all-gather.5.cloned.1.call-start = ((), (), s32[]{:S(2)}) async-start(), calls=%async_computation.1 | async-start | bytes 17825792 | tf_op jit(solution)/shard_map/all_gather | solution.py:16
  9.9 266.6 %copy-start.1 = (f32[4096]{0:T(1024)S(1)}, f32[4096]{0:T(1024)}, u32[]{:S(2)}) copy-start(f32[4096]{0:T(1024)} %param.7) | copy-start | bytes 49156
  9.9 272.9 %copy-start.2 = (f32[576]{0:T(1024)S(1)}, f32[576]{0:T(1024)}, u32[]{:S(2)}) copy-start(f32[576]{0:T(1024)} %param.6) | copy-start | bytes 6916
  277.2 14.9 %copy-start = (f32[4096]{0:T(1024)}, f32[4096]{0:T(1024)S(1)}, u32[]{:S(2)}) copy-start(f32[4096]{0:T(1024)S(1)} %get-tuple-element.9) | copy-start | bytes 49156
  282.9 9.2 %copy-start.3 = (f32[576]{0:T(1024)}, f32[576]{0:T(1024)S(1)}, u32[]{:S(2)}) copy-start(f32[576]{0:T(1024)S(1)} %multiply_add_fusion.1) | copy-start | bytes 6916
Sparse Core Ops, SparseCore 0:
  9.9 61.4 all-gather.2
  73.5 126.4 all-gather.4
where the time goes:
time: 299 us
  waiting for transfers between devices  191 us (64%)
  blocking collectives  64.5 us (22%)
  matrix products  17.7 us (6%)
  between operations  15.4 us (5%)
  other arithmetic  9.68 us (3%)
    all_gather x1, waiting for transfers between devices, body(): grads_all = lax.all_gather(out_grads, ('outer', 'row'), axis=0, tiled=True)  129 us
    all_gather x1, waiting for transfers between devices, body(): lax.all_gather(activations, ('outer', 'col'), axis=0, tiled=True)  61.4 us
    psum x1, blocking collectives, body(): lax.psum((jnp.sum(squares, axis=0), jnp.sum(row_moment)), ('outer', 'row'))  58.9 us
    dot_general x1, matrix products, body(): lax.dot_general(columns, grads_all, contract, preferred_element_type=jnp....  17.7 us
    convert_element_type x1, other arithmetic, body(): update = (gradient * factor).astype(jnp.bfloat16)  7.78 us
  transfers between devices with their start and end apart: 2, of which 2 were waited for; matrix products, arithmetic and copies ran while one was open for 0% of the time, Pallas kernels for 0%

commit v1 on v0

v1 whole, which is shorter than its diff:
```python
import functools

import jax
import jax.numpy as jnp
from jax import lax
from jax.experimental import pallas as pl
from jax.experimental.pallas import tpu as pltpu
from jax.sharding import PartitionSpec as P

D = 9216
F = 8192
STEP = 2
MESH = pl.DeviceIdType.MESH
PIECES = 2


def kernel(
    nout, nz, ncol, scale, decay,
    a_ref, g_ref, rm_ref, cm_ref,
    grad_hbm, nr_ref, nc_ref, mt_ref,
    gs, av, acc, rowp, colbuf, colz, rowbuf, totz, toto,
    g_recv, zp_send, zm_send, y_send, p_send, a_recv, a1_send, a2_send, loc_sem, out_sem,
    c_send, c_recv, cz_send, cz_recv, r_send, r_recv, tz_send, tz_recv, to_send, to_recv,
):
    tg, width = g_ref.shape
    rows, ta = av.shape[1], av.shape[2]
    piece = width // PIECES
    o = lax.axis_index("outer")
    z = lax.axis_index("row")
    x = lax.axis_index("col")
    y, core = o // 2, o % 2
    oy = (1 - y) * 2 + core
    op = y * 2 + (1 - core)
    mate = z + 1 - 2 * (z % 2)

    def remote(src, dst, s, r, dev):
        return pltpu.make_async_remote_copy(
            src_ref=src, dst_ref=dst, send_sem=s, recv_sem=r, device_id=dev, device_id_type=MESH
        )

    barrier = pltpu.get_barrier_semaphore()
    for d in range(1, nout):
        pl.semaphore_signal(barrier, inc=1, device_id={"outer": (o + d) % nout}, device_id_type=MESH)
    for d in range(1, nz):
        pl.semaphore_signal(barrier, inc=1, device_id={"row": (z + d) % nz}, device_id_type=MESH)
    for d in range(1, ncol):
        pl.semaphore_signal(barrier, inc=1, device_id={"col": (x + d) % ncol}, device_id_type=MESH)
    pl.semaphore_wait(barrier, nout + nz + ncol - 3)

    def slot(oo, zz):
        return oo * nz + zz

    def place(s, h):
        return gs.at[pl.ds(pl.multiple_of(s * tg, tg), tg), pl.ds(h * piece, piece)]

    def g_copy(src, s, h, sem, dev):
        return remote(src, place(s, h), sem, g_recv.at[s, h], dev)

    def to_up(src, oo, zz, h):
        k = jnp.where(oo == o, zz, nz)
        return g_copy(src, slot(oo, zz), h, zp_send.at[k, h], {"row": jnp.minimum(z + 1, nz - 1)})

    def to_down(src, oo, zz, h):
        k = jnp.where(oo == o, zz, nz)
        return g_copy(src, slot(oo, zz), h, zm_send.at[k, h], {"row": jnp.maximum(z - 1, 0)})

    def to_y(src, zz, h):
        return g_copy(src, slot(o, zz), h, y_send.at[zz, h], {"outer": oy})

    def to_partner(src, oo, zz, h):
        k = jnp.where(oo == o, zz, nz + zz)
        return g_copy(src, slot(oo, zz), h, p_send.at[k, h], {"outer": op})

    def arrived(oo, zz, h):
        here = place(slot(oo, zz), h)
        to_partner(here, oo, zz, h).wait_recv()
        return here

    own = [g_ref.at[:, pl.ds(h * piece, piece)] for h in range(PIECES)]
    for h in range(PIECES):
        @pl.when(z < nz - 1)
        def _():
            to_up(own[h], o, z, h).start()

        @pl.when(z > 0)
        def _():
            to_down(own[h], o, z, h).start()

        to_y(own[h], z, h).start()
        to_partner(own[h], o, z, h).start()

    def a_first(d):
        target = (o + d) % nout
        return remote(a_ref.at[target], av.at[o * ncol + x], a1_send.at[d], a_recv.at[o * ncol + x], {"outer": target})

    def a_second(q, d):
        oo = (o + q) % nout
        k = oo * ncol + x
        src = a_ref.at[o] if q == 0 else av.at[k]
        return remote(src, av.at[k], a2_send.at[q, d], a_recv.at[k], {"col": (x + d) % ncol})

    for d in range(1, nout):
        a_first(d).start()
    for d in range(1, ncol):
        a_second(0, d).start()
    local_g = pltpu.make_async_copy(g_ref, gs.at[pl.ds(pl.multiple_of(slot(o, z) * tg, tg), tg), :], loc_sem.at[0])
    local_a = pltpu.make_async_copy(a_ref.at[o], av.at[o * ncol + x], loc_sem.at[1])
    local_g.start()
    local_a.start()

    def a_arrived(k):
        remote(av.at[k], av.at[k], a1_send.at[1], a_recv.at[k], {"outer": oy}).wait_recv()

    def y_arrived(zz, forward=False):
        for h in range(PIECES):
            here = arrived(oy, zz, h)
            to_partner(here, oy, zz, h).start()

    def extra(h, act):
        here = place(slot(oy, z), h)

        @pl.when(mate > z)
        def _():
            act(to_up(here, oy, z, h))

        @pl.when(mate < z)
        def _():
            act(to_down(here, oy, z, h))

    for s in range(1, nz):
        for h in range(PIECES):
            @pl.when(z - s >= 0)
            def _():
                here = arrived(o, z - s, h)

                @pl.when(z < nz - 1)
                def _():
                    to_up(here, o, z - s, h).start()

                @pl.when(z - s != mate)
                def _():
                    to_y(here, z - s, h).start()

                to_partner(here, o, z - s, h).start()

            @pl.when(z + s < nz)
            def _():
                here = arrived(o, z + s, h)

                @pl.when(z > 0)
                def _():
                    to_down(here, o, z + s, h).start()

                @pl.when(z + s != mate)
                def _():
                    to_y(here, z + s, h).start()

                to_partner(here, o, z + s, h).start()

        if s == 1:
            y_arrived(z)
            for q in range(1, nout):
                a_arrived(((o + q) % nout) * ncol + x)
                for d in range(1, ncol):
                    a_second(q, d).start()
        else:
            for zz in (z - (s - 1), z + (s - 1)):
                @pl.when((zz >= 0) & (zz < nz) & (zz != mate))
                def _():
                    y_arrived(zz)
        if s == max(nz - 2, 1):
            for h in range(PIECES):
                extra(h, lambda c: c.start())

    local_g.wait()
    local_a.wait()
    for d in range(1, ncol):
        for q in range(nout):
            a_arrived(((o + q) % nout) * ncol + (x + d) % ncol)
    for zz in range(nz):
        for h in range(PIECES):
            arrived(op, zz, h)
    tile = min(512, piece)
    per_piece = piece // tile

    def dots(yy, columns):
        total = None
        for k in range(2 * ncol):
            block = yy * 2 * ncol + k
            part = jnp.dot(
                av[block],
                gs[pl.ds(pl.multiple_of(block * ta, ta), ta), columns],
                preferred_element_type=jnp.float32,
            )
            total = part if total is None else total + part
        return total

    @pl.loop(0, width // tile)
    def _(j):
        columns = pl.ds(pl.multiple_of(j * tile, tile), tile)
        acc[:, columns] = dots(y, columns)

    rowp[...] = jnp.zeros_like(rowp)
    od = (1 - y) * 2 + (1 - core)
    for h in range(PIECES):
        for zz in (z - (nz - 1), z + (nz - 1)):
            @pl.when((zz >= 0) & (zz < nz) & (zz != mate))
            def _():
                here = arrived(oy, zz, h)
                to_partner(here, oy, zz, h).start()

        here = arrived(oy, mate, h)
        to_partner(here, oy, mate, h).start()
    for h in range(PIECES):
        for zz in range(nz):
            arrived(od, zz, h)

        @pl.loop(h * per_piece, (h + 1) * per_piece)
        def _(j):
            columns = pl.ds(pl.multiple_of(j * tile, tile), tile)
            grad = (acc[:, columns] + dots(1 - y, columns)) * scale
            acc[:, columns] = grad
            squares = grad * grad
            part = squares[:, :128]
            for i in range(1, tile // 128):
                part = part + squares[:, i * 128 : (i + 1) * 128]
            rowp[...] += part
            colbuf[0, :, columns] = jnp.sum(squares, axis=0, keepdims=True)

    out_copy = pltpu.make_async_copy(acc, grad_hbm, out_sem)
    out_copy.start()

    def c_first(d):
        return remote(colbuf.at[0], colbuf.at[nout - d], c_send.at[d], c_recv.at[nout - d], {"outer": (o + d) % nout})

    def c_second(d):
        return remote(colz.at[0], colz.at[nz - d], cz_send.at[d], cz_recv.at[nz - d], {"row": (z + d) % nz})

    def r_first(d):
        return remote(rowbuf.at[0], rowbuf.at[ncol - d], r_send.at[d], r_recv.at[ncol - d], {"col": (x + d) % ncol})

    def t_first(d):
        return remote(totz.at[0], totz.at[nz - d], tz_send.at[d], tz_recv.at[nz - d], {"row": (z + d) % nz})

    def t_second(d):
        return remote(toto.at[0], toto.at[nout - d], to_send.at[d], to_recv.at[nout - d], {"outer": (o + d) % nout})

    def finish(copies):
        for c in copies:
            c.wait()

    firsts = [c_first(d) for d in range(1, nout)]
    for c in firsts:
        c.start()
    rowbuf[0] = jnp.sum(jnp.transpose(rowp[...]), axis=0, keepdims=True)
    rights = [r_first(d) for d in range(1, ncol)]
    for c in rights:
        c.start()
    finish(rights)
    row_sq = rowbuf[0]
    for d in range(1, ncol):
        row_sq = row_sq + rowbuf[d]
    new_row = decay * rm_ref[...] + (1.0 - decay) * row_sq / F
    nr_ref[...] = new_row
    totz[0] = jnp.broadcast_to(jnp.sum(new_row, axis=1, keepdims=True), totz.shape[1:])
    tots = [t_first(d) for d in range(1, nz)]
    for c in tots:
        c.start()
    finish(firsts)
    col_sq = colbuf[0]
    for d in range(1, nout):
        col_sq = col_sq + colbuf[d]
    colz[0] = col_sq
    seconds = [c_second(d) for d in range(1, nz)]
    for c in seconds:
        c.start()
    finish(tots)
    total = totz[0]
    for d in range(1, nz):
        total = total + totz[d]
    toto[0] = total
    lasts = [t_second(d) for d in range(1, nout)]
    for c in lasts:
        c.start()
    finish(seconds)
    col_sq = colz[0]
    for d in range(1, nz):
        col_sq = col_sq + colz[d]
    nc_ref[...] = decay * cm_ref[...] + (1.0 - decay) * col_sq / D
    finish(lasts)
    total = toto[0]
    for d in range(1, nout):
        total = total + toto[d]
    mt_ref[...] = total

    for h in range(PIECES):
        for zz in range(nz):
            @pl.when((z < nz - 1) & (zz <= z))
            def _():
                to_up(place(slot(o, zz), h), o, zz, h).wait_send()

            @pl.when((z > 0) & (zz >= z))
            def _():
                to_down(place(slot(o, zz), h), o, zz, h).wait_send()

            @pl.when(zz != mate)
            def _():
                to_y(place(slot(o, zz), h), zz, h).wait_send()

            to_partner(place(slot(o, zz), h), o, zz, h).wait_send()
            to_partner(place(slot(oy, zz), h), oy, zz, h).wait_send()
        extra(h, lambda c: c.wait_send())
    for d in range(1, nout):
        a_first(d).wait_send()
    for q in range(nout):
        for d in range(1, ncol):
            a_second(q, d).wait_send()
    out_copy.wait()


def body(nout, nz, ncol, activations, out_grads, row_moment, col_moment):
    rows, width = row_moment.shape[0], col_moment.shape[0]
    ta, tg = activations.shape[0], out_grads.shape[0]
    tokens = ta * ncol * nout
    decay = 1.0 - STEP ** (-0.8)
    turned = activations.T.reshape(nout, rows, ta)
    f32, bf16 = jnp.float32, jnp.bfloat16
    vmem = pl.BlockSpec(memory_space=pltpu.VMEM)
    dma = pltpu.SemaphoreType.DMA
    grad, new_row, new_col, total = pl.pallas_call(
        functools.partial(kernel, nout, nz, ncol, 1.0 / tokens**0.5, decay),
        out_shape=(
            jax.ShapeDtypeStruct((rows, width), f32),
            jax.ShapeDtypeStruct((1, rows), f32),
            jax.ShapeDtypeStruct((1, width), f32),
            jax.ShapeDtypeStruct((1, 128), f32),
        ),
        in_specs=[vmem] * 4,
        out_specs=(pl.BlockSpec(memory_space=pl.ANY), vmem, vmem, vmem),
        scratch_shapes=[
            pltpu.VMEM((tokens, width), bf16),
            pltpu.VMEM((nout * ncol, rows, ta), bf16),
            pltpu.VMEM((rows, width), f32),
            pltpu.VMEM((rows, 128), f32),
            pltpu.VMEM((nout, 1, width), f32),
            pltpu.VMEM((nz, 1, width), f32),
            pltpu.VMEM((ncol, 1, rows), f32),
            pltpu.VMEM((nz, 1, 128), f32),
            pltpu.VMEM((nout, 1, 128), f32),
            dma((nout * nz, PIECES)),
            dma((nz + 1, PIECES)),
            dma((nz + 1, PIECES)),
            dma((nz, PIECES)),
            dma((2 * nz, PIECES)),
            dma((nout * ncol,)),
            dma((nout,)),
            dma((nout, ncol)),
            dma((2,)),
            dma,
            dma((nout,)), dma((nout,)),
            dma((nz,)), dma((nz,)),
            dma((ncol,)), dma((ncol,)),
            dma((nz,)), dma((nz,)),
            dma((nout,)), dma((nout,)),
        ],
        compiler_params=pltpu.CompilerParams(
            collective_id=0, has_side_effects=True, vmem_limit_bytes=56 * 1024 * 1024
        ),
    )(turned, out_grads, row_moment.reshape(1, rows), col_moment.reshape(1, width))
    factor = lax.rsqrt(new_row.reshape(rows)[:, None] * new_col * (D / total[0, 0]))
    update = (grad * factor).astype(bf16)
    return (update, new_row.reshape(rows), new_col.reshape(width))


def solution(mesh):
    nout, nz, ncol = mesh.shape["outer"], mesh.shape["row"], mesh.shape["col"]
    return jax.shard_map(
        functools.partial(body, nout, nz, ncol),
        mesh=mesh,
        in_specs=(
            P(("outer", "col"), "row"),
            P(("outer", "row"), "col"),
            P(("row", "outer")),
            P("col"),
        ),
        out_specs=(P(("row", "outer"), "col"), P(("row", "outer")), P("col")),
        check_vma=False,
    )
```

time: 299 us -> 130 us (0.43)
  waiting for transfers between devices: 191 us -> 0 us
  Pallas kernels: 0 us -> 116 us
  blocking collectives: 64.5 us -> 0 us
  matrix products: 17.7 us -> 0 us
  between operations: 15.4 us -> 1.39 us
  local copies, waits for them, and re-layouts: 0.01 us -> 4.26 us
    all_gather x2 -> x0, waiting for transfers between devices: 190 us -> none  [the longest x1 129 us: body(): grads_all = lax.all_gather(out_grads, ('outer', 'row'), axis=0, tiled=True)]
    pallas_call x0 -> x1, Pallas kernels: none -> 116 us  [body(): pl.pallas_call(functools.partial(kernel, nout, nz, ncol, 1.0 / tokens **...]
    psum x2 -> x0, blocking collectives: 64.5 us -> none  [the longest x1 58.9 us: body(): lax.psum((jnp.sum(squares, axis=0), jnp.sum(row_moment)), ('outer', 'row'))]
    dot_general x1 -> x0, matrix products: 17.7 us -> none  [body(): lax.dot_general(columns, grads_all, contract, preferred_element_type=jnp....]
  transfers between devices with their start and end apart: 2 -> 0, of which waited for: 2 -> 0; matrix products, arithmetic and copies ran while one was open for 0% -> 0% of each run, Pallas kernels for 0% -> 0%
where the time goes in v1:
time: 130 us; the launch traced here: 129 us
  Pallas kernels  116 us (89%)
  other arithmetic  8.28 us (6%)
  local copies, waits for them, and re-layouts  4.26 us (3%)
  between operations  1.39 us (1%)
    pallas_call x1, Pallas kernels, body(): pl.pallas_call(functools.partial(kernel, nout, nz, ncol, 1.0 / tokens **...  116 us
    convert_element_type x1, other arithmetic, body(): update = (grad * factor).astype(bf16)  7.59 us

profile of v1, /device:TPU:0, one launch (start us, length us, event | category | flops | bytes accessed | tf_op | source)
XLA Modules:
  0.0 129.4 jit_solution(502329123246036540)
XLA Ops:
  0.6 1.3 reshape.21.rm_ref
  1.9 2.4 %copy.7 = bf16[2304,256]{1,0:T(8,128)(2,1)} copy(bf16[2304,256]{0,1:T(8,128)(2,1)} %bitcast.7) | data formatting | bytes 2359296 | tf_op jit(solution)/shard_map/transpose | solution.py:326
  4.3 115.5 %shard_map.67 = (f32[576,4096]{1,0:T(8,128)}, f32[1,576]{1,0:T(1,128)}, f32[1,4096]{1,0:T(1,128)}, f32[1,128]{1,0:T(1,128)}) custom-call(bf16[4,576,256]{2,1,0:T(8,128)(2,1)} %bitcast.6, bf16[128,4096]{1,0:T(8,128)(2,1)} %g_ref.1, f32[1,576]{1,0:T(1,128)} %reshape.21.rm_ref, f32[1,4096]{1,0:T(1,128)} %bitcast.10), custom_call_target="tpu_custom_call" | custom-call | tf_op jit(solution)/shard_map/pallas_call | solution.py:330
  119.8 0.0 copy-start
  120.5 0.7 reduce
  121.2 0.0 copy-start.1
  121.2 7.6 %multiply_convert_fusion = bf16[576,4096]{1,0:T(8,128)(2,1)} fusion(f32[576,4096]{1,0:T(8,128)} %get-tuple-element.7, f32[]{:T(128)} %bitcast.4, f32[4096]{0:T(1024)} %bitcast.8, f32[576]{0:T(1024)S(1)} %reduce), kind=kLoop, calls=%fused_computation | loop fusion | flops 9437184 | bytes 14174468 | tf_op jit(solution)/shard_map/convert_element_type | solution.py:371
  128.8 0.0 copy-done
  128.8 0.6 copy.9
  129.4 0.0 copy-done.1
Async XLA Ops:
  119.8 9.0 %copy-start = (f32[1,4096]{1,0:T(1,128)S(1)}, f32[1,4096]{1,0:T(1,128)}, u32[]{:S(2)}) copy-start(f32[1,4096]{1,0:T(1,128)} %get-tuple-element.9) | copy-start | bytes 49156
  121.2 8.2 %copy-start.1 = (f32[576]{0:T(1024)}, f32[576]{0:T(1024)S(1)}, u32[]{:S(2)}) copy-start(f32[576]{0:T(1024)S(1)} %reduce) | copy-start | bytes 6916

commit v2 on v1

--- a/solution.py
+++ b/solution.py
@@ -11,7 +11,8 @@
 F = 8192
 STEP = 2
 MESH = pl.DeviceIdType.MESH
-PIECES = 2
+PIECES = 4
+BY_Y = 1
 
 
 def kernel(
@@ -137,7 +138,7 @@
                 def _():
                     to_up(here, o, z - s, h).start()
 
-                @pl.when(z - s != mate)
+                @pl.when((z - s != mate) | (h < BY_Y))
                 def _():
                     to_y(here, z - s, h).start()
 
@@ -151,7 +152,7 @@
                 def _():
                     to_down(here, o, z + s, h).start()
 
-                @pl.when(z + s != mate)
+                @pl.when((z + s != mate) | (h < BY_Y))
                 def _():
                     to_y(here, z + s, h).start()
 
@@ -163,13 +164,13 @@
                 a_arrived(((o + q) % nout) * ncol + x)
                 for d in range(1, ncol):
                     a_second(q, d).start()
-        else:
+        elif s < nz - 1:
             for zz in (z - (s - 1), z + (s - 1)):
                 @pl.when((zz >= 0) & (zz < nz) & (zz != mate))
                 def _():
                     y_arrived(zz)
         if s == max(nz - 2, 1):
-            for h in range(PIECES):
+            for h in range(BY_Y, PIECES):
                 extra(h, lambda c: c.start())
 
     local_g.wait()
@@ -202,16 +203,7 @@
 
     rowp[...] = jnp.zeros_like(rowp)
     od = (1 - y) * 2 + (1 - core)
-    for h in range(PIECES):
-        for zz in (z - (nz - 1), z + (nz - 1)):
-            @pl.when((zz >= 0) & (zz < nz) & (zz != mate))
-            def _():
-                here = arrived(oy, zz, h)
-                to_partner(here, oy, zz, h).start()
-
-        here = arrived(oy, mate, h)
-        to_partner(here, oy, mate, h).start()
-    for h in range(PIECES):
+    def finish_piece(h):
         for zz in range(nz):
             arrived(od, zz, h)
 
@@ -227,6 +219,21 @@
             rowp[...] += part
             colbuf[0, :, columns] = jnp.sum(squares, axis=0, keepdims=True)
 
+    for h in range(PIECES):
+        for s in range(nz - 2, nz):
+            if s > 1 or (s == 1 and nz == 2):
+                for zz in (z - s, z + s):
+                    @pl.when((zz >= 0) & (zz < nz) & (zz != mate))
+                    def _():
+                        here = arrived(oy, zz, h)
+                        to_partner(here, oy, zz, h).start()
+
+        here = arrived(oy, mate, h)
+        to_partner(here, oy, mate, h).start()
+        if h > 0:
+            finish_piece(h - 1)
+    finish_piece(PIECES - 1)
+
     out_copy = pltpu.make_async_copy(acc, grad_hbm, out_sem)
     out_copy.start()
 
@@ -303,13 +310,14 @@
             def _():
                 to_down(place(slot(o, zz), h), o, zz, h).wait_send()
 
-            @pl.when(zz != mate)
+            @pl.when((zz != mate) | (h < BY_Y))
             def _():
                 to_y(place(slot(o, zz), h), zz, h).wait_send()
 
             to_partner(place(slot(o, zz), h), o, zz, h).wait_send()
             to_partner(place(slot(oy, zz), h), oy, zz, h).wait_send()
-        extra(h, lambda c: c.wait_send())
+        if h >= BY_Y:
+            extra(h, lambda c: c.wait_send())
     for d in range(1, nout):
         a_first(d).wait_send()
     for q in range(nout):
@@ -364,7 +372,7 @@
             dma((nout,)), dma((nout,)),
         ],
         compiler_params=pltpu.CompilerParams(
-            collective_id=0, has_side_effects=True, vmem_limit_bytes=56 * 1024 * 1024
+            collective_id=0, has_side_effects=True, vmem_limit_bytes=44 * 1024 * 1024
         ),
     )(turned, out_grads, row_moment.reshape(1, rows), col_moment.reshape(1, width))
     factor = lax.rsqrt(new_row.reshape(rows)[:, None] * new_col * (D / total[0, 0]))

time: 130 us -> 121 us (0.931)
  Pallas kernels: 116 us -> 107 us
    pallas_call x1, Pallas kernels: 116 us -> 107 us  [body(): pl.pallas_call(functools.partial(kernel, nout, nz, ncol, 1.0 / tokens **...]
    unnamed x5 -> x7, local copies, waits for them, and re-layouts: 0.62 us -> 2.55 us
where the time goes in v2:
time: 121 us; the launch traced here: 120 us
  Pallas kernels  107 us (88%)
  other arithmetic  7.6 us (6%)
  local copies, waits for them, and re-layouts  4.81 us (4%)
    pallas_call x1, Pallas kernels, body(): pl.pallas_call(functools.partial(kernel, nout, nz, ncol, 1.0 / tokens **...  107 us
    convert_element_type x1, other arithmetic, body(): update = (grad * factor).astype(bf16)  7.59 us
    unnamed x7, local copies, waits for them, and re-layouts  2.55 us

profile of v2, /device:TPU:0, one launch (start us, length us, event | category | flops | bytes accessed | tf_op | source)
XLA Modules:
  0.0 120.2 jit_solution(6376540009276445627)
XLA Ops:
  0.6 0.7 reshape.21.rm_ref
  1.3 1.6 %copy.7 = bf16[2304,256]{1,0:T(8,128)(2,1)S(1)} copy(bf16[2304,256]{0,1:T(8,128)(2,1)} %bitcast.11) | data formatting | bytes 2359296 | tf_op jit(solution)/shard_map/transpose | solution.py:334
  2.9 0.0 copy-start
  2.9 1.2 %copy-done = bf16[128,4096]{1,0:T(8,128)(2,1)S(1)} copy-done((bf16[128,4096]{1,0:T(8,128)(2,1)S(1)}, bf16[128,4096]{1,0:T(8,128)(2,1)}, u32[]{:S(2)}) %copy-start) | copy-done | bytes 1048600
  4.1 0.0 copy-start.1
  4.1 0.7 copy-done.1
  4.8 107.1 %shard_map.67 = (f32[576,4096]{1,0:T(8,128)}, f32[1,576]{1,0:T(1,128)S(1)}, f32[1,4096]{1,0:T(1,128)S(1)}, f32[1,128]{1,0:T(1,128)S(1)}) custom-call(bf16[4,576,256]{2,1,0:T(8,128)(2,1)S(1)} %bitcast.6, bf16[128,4096]{1,0:T(8,128)(2,1)S(1)} %copy-done, f32[1,576]{1,0:T(1,128)S(1)} %reshape.21.rm_ref, f32[1,4096]{1,0:T(1,128)S(1)} %bitcast.9), custom_call_target="tpu_custom_call" | custom-call | tf_op jit(solution)/shard_map/pallas_call | solution.py:338
  112.0 0.0 copy-start.2
  112.0 7.6 %multiply_convert_fusion = bf16[576,4096]{1,0:T(8,128)(2,1)} fusion(f32[576,4096]{1,0:T(8,128)} %get-tuple-element.7, f32[]{:T(128)} %bitcast.4, f32[4096]{0:T(1024)S(1)} %bitcast.7, f32[576]{0:T(1024)S(1)} %reduce), kind=kLoop, calls=%fused_computation | loop fusion | flops 9437184 | bytes 14174468 | tf_op jit(solution)/shard_map/convert_element_type | solution.py:379
  119.6 0.6 copy.9
  120.2 0.0 copy-done.2
  (1 shorter events, 0.0 us)
Async XLA Ops:
  2.9 1.2 %copy-start = (bf16[128,4096]{1,0:T(8,128)(2,1)S(1)}, bf16[128,4096]{1,0:T(8,128)(2,1)}, u32[]{:S(2)}) copy-start(bf16[128,4096]{1,0:T(8,128)(2,1)} %g_ref.1) | copy-start | bytes 3145732
  4.1 0.7 copy-start.1
  112.0 8.2 %copy-start.2 = (f32[576]{0:T(1024)}, f32[576]{0:T(1024)S(1)}, u32[]{:S(2)}) copy-start(f32[576]{0:T(1024)S(1)} %reduce) | copy-start | bytes 6916

commit v3 on v2

--- a/solution.py
+++ b/solution.py
@@ -18,9 +18,9 @@
 def kernel(
     nout, nz, ncol, scale, decay,
     a_ref, g_ref, rm_ref, cm_ref,
-    grad_hbm, nr_ref, nc_ref, mt_ref,
-    gs, av, acc, rowp, colbuf, colz, rowbuf, totz, toto,
-    g_recv, zp_send, zm_send, y_send, p_send, a_recv, a1_send, a2_send, loc_sem, out_sem,
+    acc, nr_ref, nrc_ref, nc_ref, mt_ref,
+    gs, av, rowp, colbuf, colz, rowbuf, totz, toto,
+    g_recv, zp_send, zm_send, y_send, p_send, a_recv, a1_send, a2_send, loc_sem,
     c_send, c_recv, cz_send, cz_recv, r_send, r_recv, tz_send, tz_recv, to_send, to_recv,
 ):
     tg, width = g_ref.shape
@@ -42,11 +42,19 @@
     barrier = pltpu.get_barrier_semaphore()
     for d in range(1, nout):
         pl.semaphore_signal(barrier, inc=1, device_id={"outer": (o + d) % nout}, device_id_type=MESH)
-    for d in range(1, nz):
-        pl.semaphore_signal(barrier, inc=1, device_id={"row": (z + d) % nz}, device_id_type=MESH)
+
+    @pl.when(z > 0)
+    def _():
+        pl.semaphore_signal(barrier, inc=1, device_id={"row": jnp.maximum(z - 1, 0)}, device_id_type=MESH)
+
+    @pl.when(z < nz - 1)
+    def _():
+        pl.semaphore_signal(barrier, inc=1, device_id={"row": jnp.minimum(z + 1, nz - 1)}, device_id_type=MESH)
+
     for d in range(1, ncol):
         pl.semaphore_signal(barrier, inc=1, device_id={"col": (x + d) % ncol}, device_id_type=MESH)
-    pl.semaphore_wait(barrier, nout + nz + ncol - 3)
+    ends = jnp.where(z > 0, 1, 0) + jnp.where(z < nz - 1, 1, 0)
+    pl.semaphore_wait(barrier, nout + ncol - 2 + ends)
 
     def slot(oo, zz):
         return oo * nz + zz
@@ -234,9 +242,6 @@
             finish_piece(h - 1)
     finish_piece(PIECES - 1)
 
-    out_copy = pltpu.make_async_copy(acc, grad_hbm, out_sem)
-    out_copy.start()
-
     def c_first(d):
         return remote(colbuf.at[0], colbuf.at[nout - d], c_send.at[d], c_recv.at[nout - d], {"outer": (o + d) % nout})
 
@@ -247,10 +252,12 @@
         return remote(rowbuf.at[0], rowbuf.at[ncol - d], r_send.at[d], r_recv.at[ncol - d], {"col": (x + d) % ncol})
 
     def t_first(d):
-        return remote(totz.at[0], totz.at[nz - d], tz_send.at[d], tz_recv.at[nz - d], {"row": (z + d) % nz})
-
-    def t_second(d):
         return remote(toto.at[0], toto.at[nout - d], to_send.at[d], to_recv.at[nout - d], {"outer": (o + d) % nout})
+
+    def t_second(d, e):
+        k = ((nz - d) % nz) * ncol + (ncol - e) % ncol
+        dev = {"row": (z + d) % nz, "col": (x + e) % ncol}
+        return remote(totz.at[0], totz.at[k], tz_send.at[d * ncol + e], tz_recv.at[k], dev)
 
     def finish(copies):
         for c in copies:
@@ -259,18 +266,14 @@
     firsts = [c_first(d) for d in range(1, nout)]
     for c in firsts:
         c.start()
-    rowbuf[0] = jnp.sum(jnp.transpose(rowp[...]), axis=0, keepdims=True)
+    mine = jnp.sum(jnp.transpose(rowp[...]), axis=0, keepdims=True)
+    rowbuf[0] = mine
     rights = [r_first(d) for d in range(1, ncol)]
     for c in rights:
         c.start()
-    finish(rights)
-    row_sq = rowbuf[0]
-    for d in range(1, ncol):
-        row_sq = row_sq + rowbuf[d]
-    new_row = decay * rm_ref[...] + (1.0 - decay) * row_sq / F
-    nr_ref[...] = new_row
-    totz[0] = jnp.broadcast_to(jnp.sum(new_row, axis=1, keepdims=True), totz.shape[1:])
-    tots = [t_first(d) for d in range(1, nz)]
+    share = (decay / ncol) * rm_ref[...] + ((1.0 - decay) / F) * mine
+    toto[0] = jnp.broadcast_to(jnp.sum(share, axis=1, keepdims=True), toto.shape[1:])
+    tots = [t_first(d) for d in range(1, nout)]
     for c in tots:
         c.start()
     finish(firsts)
@@ -278,26 +281,33 @@
     for d in range(1, nout):
         col_sq = col_sq + colbuf[d]
     colz[0] = col_sq
+    finish(rights)
     seconds = [c_second(d) for d in range(1, nz)]
     for c in seconds:
         c.start()
     finish(tots)
-    total = totz[0]
-    for d in range(1, nz):
-        total = total + totz[d]
-    toto[0] = total
-    lasts = [t_second(d) for d in range(1, nout)]
+    total = toto[0]
+    for d in range(1, nout):
+        total = total + toto[d]
+    totz[0] = total
+    lasts = [t_second(d, e) for d in range(nz) for e in range(ncol) if d + e > 0]
     for c in lasts:
         c.start()
+    row_sq = rowbuf[0]
+    for d in range(1, ncol):
+        row_sq = row_sq + rowbuf[d]
+    new_row = decay * rm_ref[...] + (1.0 - decay) * row_sq / F
+    nr_ref[...] = new_row
+    nrc_ref[...] = jnp.transpose(jnp.broadcast_to(new_row, (128, new_row.shape[1])))
     finish(seconds)
     col_sq = colz[0]
     for d in range(1, nz):
         col_sq = col_sq + colz[d]
     nc_ref[...] = decay * cm_ref[...] + (1.0 - decay) * col_sq / D
     finish(lasts)
-    total = toto[0]
-    for d in range(1, nout):
-        total = total + toto[d]
+    total = totz[0]
+    for k in range(1, nz * ncol):
+        total = total + totz[k]
     mt_ref[...] = total
 
     for h in range(PIECES):
@@ -323,7 +333,13 @@
     for q in range(nout):
         for d in range(1, ncol):
             a_second(q, d).wait_send()
-    out_copy.wait()
+
+
+def update_kernel(step, grad_ref, nr_ref, nc_ref, mt_ref, out_ref):
+    here = pl.ds(pl.multiple_of(pl.program_id(0) * step, step), step)
+    scale = D / mt_ref[0, 0]
+    factor = lax.rsqrt(nr_ref[here, :1] * nc_ref[...] * scale)
+    out_ref[...] = (grad_ref[here, :] * factor).astype(out_ref.dtype)
 
 
 def body(nout, nz, ncol, activations, out_grads, row_moment, col_moment):
@@ -335,25 +351,25 @@
     f32, bf16 = jnp.float32, jnp.bfloat16
     vmem = pl.BlockSpec(memory_space=pltpu.VMEM)
     dma = pltpu.SemaphoreType.DMA
-    grad, new_row, new_col, total = pl.pallas_call(
+    grad, new_row, turned_row, new_col, total = pl.pallas_call(
         functools.partial(kernel, nout, nz, ncol, 1.0 / tokens**0.5, decay),
         out_shape=(
-            jax.ShapeDtypeStruct((rows, width), f32),
+            pltpu.VMEM((rows, width), f32),
             jax.ShapeDtypeStruct((1, rows), f32),
+            pltpu.VMEM((rows, 128), f32),
             jax.ShapeDtypeStruct((1, width), f32),
             jax.ShapeDtypeStruct((1, 128), f32),
         ),
-        in_specs=[vmem] * 4,
-        out_specs=(pl.BlockSpec(memory_space=pl.ANY), vmem, vmem, vmem),
+        in_specs=[vmem, pl.BlockSpec(memory_space=pl.ANY), vmem, vmem],
+        out_specs=(vmem,) * 5,
         scratch_shapes=[
             pltpu.VMEM((tokens, width), bf16),
             pltpu.VMEM((nout * ncol, rows, ta), bf16),
-            pltpu.VMEM((rows, width), f32),
             pltpu.VMEM((rows, 128), f32),
             pltpu.VMEM((nout, 1, width), f32),
             pltpu.VMEM((nz, 1, width), f32),
             pltpu.VMEM((ncol, 1, rows), f32),
-            pltpu.VMEM((nz, 1, 128), f32),
+            pltpu.VMEM((nz * ncol, 1, 128), f32),
             pltpu.VMEM((nout, 1, 128), f32),
             dma((nout * nz, PIECES)),
             dma((nz + 1, PIECES)),
@@ -364,19 +380,26 @@
             dma((nout,)),
             dma((nout, ncol)),
             dma((2,)),
-            dma,
             dma((nout,)), dma((nout,)),
             dma((nz,)), dma((nz,)),
             dma((ncol,)), dma((ncol,)),
-            dma((nz,)), dma((nz,)),
+            dma((nz * ncol,)), dma((nz * ncol,)),
             dma((nout,)), dma((nout,)),
         ],
         compiler_params=pltpu.CompilerParams(
             collective_id=0, has_side_effects=True, vmem_limit_bytes=44 * 1024 * 1024
         ),
     )(turned, out_grads, row_moment.reshape(1, rows), col_moment.reshape(1, width))
-    factor = lax.rsqrt(new_row.reshape(rows)[:, None] * new_col * (D / total[0, 0]))
-    update = (grad * factor).astype(bf16)
+    parts = next(n for n in (4, 3, 2, 1) if n == 1 or rows % (n * 16) == 0)
+    step = rows // parts
+    update = pl.pallas_call(
+        functools.partial(update_kernel, step),
+        grid=(parts,),
+        out_shape=jax.ShapeDtypeStruct((rows, width), bf16),
+        in_specs=[vmem] * 4,
+        out_specs=pl.BlockSpec((step, width), lambda i: (i, 0)),
+        compiler_params=pltpu.CompilerParams(vmem_limit_bytes=24 * 1024 * 1024),
+    )(grad, turned_row, new_col, total)
     return (update, new_row.reshape(rows), new_col.reshape(width))
 
 

time: 121 us -> 117 us (0.967)
  other arithmetic: 7.6 us -> 0.6 us
  Pallas kernels: 107 us -> 111 us
    convert_element_type x1 -> x0, other arithmetic: 7.59 us -> none  [body(): update = (grad * factor).astype(bf16)]
    pallas_call x0 -> x1, Pallas kernels: none -> 4.5 us  [body(): pl.pallas_call(functools.partial(update_kernel, step), grid=(parts,), out...]
    unnamed x7 -> x3, local copies, waits for them, and re-layouts: 2.55 us -> 1.32 us
where the time goes in v3:
time: 117 us
  Pallas kernels  111 us (95%)
  local copies, waits for them, and re-layouts  4.38 us (4%)
    pallas_call x1, Pallas kernels, body(): pl.pallas_call(functools.partial(kernel, nout, nz, ncol, 1.0 / tokens **...  107 us
    pallas_call x1, Pallas kernels, body(): pl.pallas_call(functools.partial(update_kernel, step), grid=(parts,), out...  4.5 us
    transpose x1, local copies, waits for them, and re-layouts, body(): turned = activations.T.reshape(nout, rows, ta)  2.37 us

profile of v3, /device:TPU:0, one launch (start us, length us, event | category | flops | bytes accessed | tf_op | source)
XLA Modules:
  0.0 117.1 jit_solution(628532515950725878)
XLA Ops:
  0.6 0.7 reshape.22.rm_ref
  1.3 2.4 %copy.7 = bf16[2304,256]{1,0:T(8,128)(2,1)} copy(bf16[2304,256]{0,1:T(8,128)(2,1)} %bitcast.7) | data formatting | bytes 2359296 | tf_op jit(solution)/shard_map/transpose | solution.py:350
  3.7 0.0 copy-start
  3.7 0.7 copy-done
  4.4 107.0 %shard_map.67 = (f32[576,4096]{1,0:T(8,128)S(1)}, f32[1,576]{1,0:T(1,128)S(1)}, f32[576,128]{1,0:T(8,128)S(1)}, f32[1,4096]{1,0:T(1,128)S(1)}, f32[1,128]{1,0:T(1,128)S(1)}) custom-call(bf16[4,576,256]{2,1,0:T(8,128)(2,1)} %bitcast.6, bf16[128,4096]{1,0:T(8,128)(2,1)} %g_ref.1, f32[1,576]{1,0:T(1,128)S(1)} %reshape.22.rm_ref, f32[1,4096]{1,0:T(1,128)S(1)} %bitcast.5), custom_call_target="tpu_custom_call" | custom-call | tf_op jit(solution)/shard_map/pallas_call | solution.py:354
  111.4 4.5 %shard_map.68 = bf16[576,4096]{1,0:T(8,128)(2,1)} custom-call(f32[576,4096]{1,0:T(8,128)S(1)} %get-tuple-element.8.grad_ref, f32[576,128]{1,0:T(8,128)S(1)} %get-tuple-element.9.nr_ref, f32[1,4096]{1,0:T(1,128)S(1)} %get-tuple-element.10.nc_ref, f32[1,128]{1,0:T(1,128)S(1)} %get-tuple-element.11.mt_ref), custom_call_target="tpu_custom_call" | custom-call | tf_op jit(solution)/shard_map/pallas_call | solution.py:395
  115.9 0.6 reduce
  116.5 0.6 copy.9
Async XLA Ops:
  3.7 0.7 copy-start

commit v4 on v3

--- a/solution.py
+++ b/solution.py
@@ -17,9 +17,9 @@
 
 def kernel(
     nout, nz, ncol, scale, decay,
-    a_ref, g_ref, rm_ref, cm_ref,
+    raw_ref, g_ref, rm_ref, cm_ref,
     acc, nr_ref, nrc_ref, nc_ref, mt_ref,
-    gs, av, rowp, colbuf, colz, rowbuf, totz, toto,
+    gs, av, raw, a_ref, rowp, colbuf, colz, rowbuf, totz, toto,
     g_recv, zp_send, zm_send, y_send, p_send, a_recv, a1_send, a2_send, loc_sem,
     c_send, c_recv, cz_send, cz_recv, r_send, r_recv, tz_send, tz_recv, to_send, to_recv,
 ):
@@ -39,6 +39,8 @@
             src_ref=src, dst_ref=dst, send_sem=s, recv_sem=r, device_id=dev, device_id_type=MESH
         )
 
+    load_a = pltpu.make_async_copy(raw_ref, raw, loc_sem.at[2])
+    load_a.start()
     barrier = pltpu.get_barrier_semaphore()
     for d in range(1, nout):
         pl.semaphore_signal(barrier, inc=1, device_id={"outer": (o + d) % nout}, device_id_type=MESH)
@@ -108,14 +110,13 @@
         src = a_ref.at[o] if q == 0 else av.at[k]
         return remote(src, av.at[k], a2_send.at[q, d], a_recv.at[k], {"col": (x + d) % ncol})
 
-    for d in range(1, nout):
-        a_first(d).start()
-    for d in range(1, ncol):
-        a_second(0, d).start()
     local_g = pltpu.make_async_copy(g_ref, gs.at[pl.ds(pl.multiple_of(slot(o, z) * tg, tg), tg), :], loc_sem.at[0])
     local_a = pltpu.make_async_copy(a_ref.at[o], av.at[o * ncol + x], loc_sem.at[1])
     local_g.start()
-    local_a.start()
+    load_a.wait()
+    turned = jnp.transpose(raw[...])
+    for k in range(nout):
+        a_ref[k] = turned[k * rows : (k + 1) * rows]
 
     def a_arrived(k):
         remote(av.at[k], av.at[k], a1_send.at[1], a_recv.at[k], {"outer": oy}).wait_recv()
@@ -165,6 +166,13 @@
                     to_y(here, z + s, h).start()
 
                 to_partner(here, o, z + s, h).start()
+
+            if s == 1 and h == 1:
+                for d in range(1, nout):
+                    a_first(d).start()
+                for d in range(1, ncol):
+                    a_second(0, d).start()
+                local_a.start()
 
         if s == 1:
             y_arrived(z)
@@ -271,7 +279,7 @@
     rights = [r_first(d) for d in range(1, ncol)]
     for c in rights:
         c.start()
-    share = (decay / ncol) * rm_ref[...] + ((1.0 - decay) / F) * mine
+    share = (decay / ncol) * rm_ref[...].reshape(1, rows) + ((1.0 - decay) / F) * mine
     toto[0] = jnp.broadcast_to(jnp.sum(share, axis=1, keepdims=True), toto.shape[1:])
     tots = [t_first(d) for d in range(1, nout)]
     for c in tots:
@@ -296,14 +304,14 @@
     row_sq = rowbuf[0]
     for d in range(1, ncol):
         row_sq = row_sq + rowbuf[d]
-    new_row = decay * rm_ref[...] + (1.0 - decay) * row_sq / F
+    new_row = decay * rm_ref[...].reshape(1, rows) + (1.0 - decay) * row_sq / F
     nr_ref[...] = new_row
     nrc_ref[...] = jnp.transpose(jnp.broadcast_to(new_row, (128, new_row.shape[1])))
     finish(seconds)
     col_sq = colz[0]
     for d in range(1, nz):
         col_sq = col_sq + colz[d]
-    nc_ref[...] = decay * cm_ref[...] + (1.0 - decay) * col_sq / D
+    nc_ref[...] = decay * cm_ref[...].reshape(1, width) + (1.0 - decay) * col_sq / D
     finish(lasts)
     total = totz[0]
     for k in range(1, nz * ncol):
@@ -335,11 +343,17 @@
             a_second(q, d).wait_send()
 
 
-def update_kernel(step, grad_ref, nr_ref, nc_ref, mt_ref, out_ref):
+def update_kernel(step, grad_ref, nr_ref, nc_ref, mt_ref, flat_ref, out_ref, row_ref, col_ref):
     here = pl.ds(pl.multiple_of(pl.program_id(0) * step, step), step)
     scale = D / mt_ref[0, 0]
-    factor = lax.rsqrt(nr_ref[here, :1] * nc_ref[...] * scale)
-    out_ref[...] = (grad_ref[here, :] * factor).astype(out_ref.dtype)
+    by_row = lax.rsqrt(nr_ref[here, :1])
+    by_col = lax.rsqrt(nc_ref[...] * scale)
+    @pl.when(pl.program_id(0) == 0)
+    def _():
+        row_ref[...] = flat_ref[...].reshape(row_ref.shape)
+        col_ref[...] = nc_ref[...].reshape(col_ref.shape)
+
+    out_ref[...] = (grad_ref[here, :] * by_row * by_col).astype(out_ref.dtype)
 
 
 def body(nout, nz, ncol, activations, out_grads, row_moment, col_moment):
@@ -347,7 +361,6 @@
     ta, tg = activations.shape[0], out_grads.shape[0]
     tokens = ta * ncol * nout
     decay = 1.0 - STEP ** (-0.8)
-    turned = activations.T.reshape(nout, rows, ta)
     f32, bf16 = jnp.float32, jnp.bfloat16
     vmem = pl.BlockSpec(memory_space=pltpu.VMEM)
     dma = pltpu.SemaphoreType.DMA
@@ -360,11 +373,13 @@
             jax.ShapeDtypeStruct((1, width), f32),
             jax.ShapeDtypeStruct((1, 128), f32),
         ),
-        in_specs=[vmem, pl.BlockSpec(memory_space=pl.ANY), vmem, vmem],
+        in_specs=[pl.BlockSpec(memory_space=pl.ANY)] * 2 + [vmem] * 2,
         out_specs=(vmem,) * 5,
         scratch_shapes=[
             pltpu.VMEM((tokens, width), bf16),
             pltpu.VMEM((nout * ncol, rows, ta), bf16),
+            pltpu.VMEM(activations.shape, bf16),
+            pltpu.VMEM((nout, rows, ta), bf16),
             pltpu.VMEM((rows, 128), f32),
             pltpu.VMEM((nout, 1, width), f32),
             pltpu.VMEM((nz, 1, width), f32),
@@ -379,7 +394,7 @@
             dma((nout * ncol,)),
             dma((nout,)),
             dma((nout, ncol)),
-            dma((2,)),
+            dma((3,)),
             dma((nout,)), dma((nout,)),
             dma((nz,)), dma((nz,)),
             dma((ncol,)), dma((ncol,)),
@@ -389,18 +404,22 @@
         compiler_params=pltpu.CompilerParams(
             collective_id=0, has_side_effects=True, vmem_limit_bytes=44 * 1024 * 1024
         ),
-    )(turned, out_grads, row_moment.reshape(1, rows), col_moment.reshape(1, width))
+    )(activations, out_grads, row_moment, col_moment)
     parts = next(n for n in (4, 3, 2, 1) if n == 1 or rows % (n * 16) == 0)
     step = rows // parts
-    update = pl.pallas_call(
+    update, flat_row, flat_col = pl.pallas_call(
         functools.partial(update_kernel, step),
         grid=(parts,),
-        out_shape=jax.ShapeDtypeStruct((rows, width), bf16),
-        in_specs=[vmem] * 4,
-        out_specs=pl.BlockSpec((step, width), lambda i: (i, 0)),
+        out_shape=(
+            jax.ShapeDtypeStruct((rows, width), bf16),
+            jax.ShapeDtypeStruct((rows,), f32),
+            jax.ShapeDtypeStruct((width,), f32),
+        ),
+        in_specs=[vmem] * 5,
+        out_specs=(pl.BlockSpec((step, width), lambda i: (i, 0)), vmem, vmem),
         compiler_params=pltpu.CompilerParams(vmem_limit_bytes=24 * 1024 * 1024),
-    )(grad, turned_row, new_col, total)
-    return (update, new_row.reshape(rows), new_col.reshape(width))
+    )(grad, turned_row, new_col, total, new_row)
+    return (update, flat_row, flat_col)
 
 
 def solution(mesh):

time: 117 us -> 115 us (0.983)
  local copies, waits for them, and re-layouts: 4.38 us -> 1.4 us
    transpose x1 -> x0, local copies, waits for them, and re-layouts: 2.37 us -> none  [body(): turned = activations.T.reshape(nout, rows, ta)]
    pallas_call x1, Pallas kernels: 107 us -> 109 us  [body(): pl.pallas_call(functools.partial(kernel, nout, nz, ncol, 1.0 / tokens **...]
    pallas_call x1, Pallas kernels: 4.5 us -> 3.18 us  [body(): pl.pallas_call(functools.partial(update_kernel, step), grid=(parts,), out...]
where the time goes in v4:
time: 115 us; the launch traced here: 114 us
  Pallas kernels  112 us (97%)
  local copies, waits for them, and re-layouts  1.4 us (1%)
    pallas_call x1, Pallas kernels, body(): pl.pallas_call(functools.partial(kernel, nout, nz, ncol, 1.0 / tokens **...  109 us
    pallas_call x1, Pallas kernels, body(): pl.pallas_call(functools.partial(update_kernel, step), grid=(parts,), out...  3.18 us

profile of v4, /device:TPU:0, one launch (start us, length us, event | category | flops | bytes accessed | tf_op | source)
XLA Modules:
  0.0 114.3 jit_solution(12039751650264031283)
XLA Ops:
  0.6 0.0 copy-start
  0.6 0.7 copy-done
  1.3 0.0 copy-start.1
  1.4 0.7 copy-done.1
  2.0 109.1 %shard_map.67 = (f32[576,4096]{1,0:T(8,128)S(1)}, f32[1,576]{1,0:T(1,128)S(1)}, f32[576,128]{1,0:T(8,128)S(1)}, f32[1,4096]{1,0:T(1,128)S(1)}, f32[1,128]{1,0:T(1,128)S(1)}) custom-call(bf16[256,2304]{1,0:T(8,128)(2,1)} %raw_ref.1, bf16[128,4096]{1,0:T(8,128)(2,1)} %g_ref.1, f32[576]{0:T(1024)S(1)} %copy-done.1, f32[4096]{0:T(1024)S(1)} %copy-done), custom_call_target="tpu_custom_call" | custom-call | tf_op jit(solution)/shard_map/pallas_call | solution.py:367
  111.1 3.2 %shard_map.68 = (bf16[576,4096]{1,0:T(8,128)(2,1)}, f32[576]{0:T(1024)}, f32[4096]{0:T(1024)}) custom-call(f32[576,4096]{1,0:T(8,128)S(1)} %get-tuple-element.8.grad_ref, f32[576,128]{1,0:T(8,128)S(1)} %get-tuple-element.9.nr_ref, f32[1,4096]{1,0:T(1,128)S(1)} %get-tuple-element.10.nc_ref, f32[1,128]{1,0:T(1,128)S(1)} %get-tuple-element.11.mt_ref, ...), custom_call_target="tpu_custom_call" | custom-call | tf_op jit(solution)/shard_map/pallas_call | solution.py:410
Async XLA Ops:
  0.6 0.7 copy-start
  1.3 0.7 copy-start.1

commit v5 on v4

--- a/solution.py
+++ b/solution.py
@@ -17,9 +17,9 @@
 
 def kernel(
     nout, nz, ncol, scale, decay,
-    raw_ref, g_ref, rm_ref, cm_ref,
+    raw_ref, g_ref, rm_hbm, cm_hbm,
     acc, nr_ref, nrc_ref, nc_ref, mt_ref,
-    gs, av, raw, a_ref, rowp, colbuf, colz, rowbuf, totz, toto,
+    gs, av, raw, a_ref, rm_ref, cm_ref, rowp, colbuf, colz, rowbuf, totz, toto,
     g_recv, zp_send, zm_send, y_send, p_send, a_recv, a1_send, a2_send, loc_sem,
     c_send, c_recv, cz_send, cz_recv, r_send, r_recv, tz_send, tz_recv, to_send, to_recv,
 ):
@@ -41,6 +41,10 @@
 
     load_a = pltpu.make_async_copy(raw_ref, raw, loc_sem.at[2])
     load_a.start()
+    load_rm = pltpu.make_async_copy(rm_hbm, rm_ref, loc_sem.at[3])
+    load_cm = pltpu.make_async_copy(cm_hbm, cm_ref, loc_sem.at[4])
+    load_rm.start()
+    load_cm.start()
     barrier = pltpu.get_barrier_semaphore()
     for d in range(1, nout):
         pl.semaphore_signal(barrier, inc=1, device_id={"outer": (o + d) % nout}, device_id_type=MESH)
@@ -104,11 +108,10 @@
         target = (o + d) % nout
         return remote(a_ref.at[target], av.at[o * ncol + x], a1_send.at[d], a_recv.at[o * ncol + x], {"outer": target})
 
-    def a_second(q, d):
-        oo = (o + q) % nout
+    def a_second(oo, d, own=False):
         k = oo * ncol + x
-        src = a_ref.at[o] if q == 0 else av.at[k]
-        return remote(src, av.at[k], a2_send.at[q, d], a_recv.at[k], {"col": (x + d) % ncol})
+        src = a_ref.at[o] if own else av.at[k]
+        return remote(src, av.at[k], a2_send.at[oo, d], a_recv.at[k], {"col": (x + d) % ncol})
 
     local_g = pltpu.make_async_copy(g_ref, gs.at[pl.ds(pl.multiple_of(slot(o, z) * tg, tg), tg), :], loc_sem.at[0])
     local_a = pltpu.make_async_copy(a_ref.at[o], av.at[o * ncol + x], loc_sem.at[1])
@@ -121,7 +124,12 @@
     def a_arrived(k):
         remote(av.at[k], av.at[k], a1_send.at[1], a_recv.at[k], {"outer": oy}).wait_recv()
 
-    def y_arrived(zz, forward=False):
+    def pass_on(oo):
+        a_arrived(oo * ncol + x)
+        for d in range(1, ncol):
+            a_second(oo, d).start()
+
+    def y_arrived(zz):
         for h in range(PIECES):
             here = arrived(oy, zz, h)
             to_partner(here, oy, zz, h).start()
@@ -167,20 +175,20 @@
 
                 to_partner(here, o, z + s, h).start()
 
-            if s == 1 and h == 1:
+            if s == 1 and h == 0:
                 for d in range(1, nout):
                     a_first(d).start()
                 for d in range(1, ncol):
-                    a_second(0, d).start()
+                    a_second(o, d, True).start()
                 local_a.start()
 
         if s == 1:
             y_arrived(z)
-            for q in range(1, nout):
-                a_arrived(((o + q) % nout) * ncol + x)
-                for d in range(1, ncol):
-                    a_second(q, d).start()
-        elif s < nz - 1:
+            pass_on(op)
+        if s == min(2, nz - 1):
+            for c in range(2):
+                pass_on((1 - y) * 2 + c)
+        if 1 < s < nz - 1:
             for zz in (z - (s - 1), z + (s - 1)):
                 @pl.when((zz >= 0) & (zz < nz) & (zz != mate))
                 def _():
@@ -191,6 +199,8 @@
 
     local_g.wait()
     local_a.wait()
+    load_rm.wait()
+    load_cm.wait()
     for d in range(1, ncol):
         for q in range(nout):
             a_arrived(((o + q) % nout) * ncol + (x + d) % ncol)
@@ -338,9 +348,9 @@
             extra(h, lambda c: c.wait_send())
     for d in range(1, nout):
         a_first(d).wait_send()
-    for q in range(nout):
+    for oo in range(nout):
         for d in range(1, ncol):
-            a_second(q, d).wait_send()
+            a_second(oo, d).wait_send()
 
 
 def update_kernel(step, grad_ref, nr_ref, nc_ref, mt_ref, flat_ref, out_ref, row_ref, col_ref):
@@ -373,13 +383,15 @@
             jax.ShapeDtypeStruct((1, width), f32),
             jax.ShapeDtypeStruct((1, 128), f32),
         ),
-        in_specs=[pl.BlockSpec(memory_space=pl.ANY)] * 2 + [vmem] * 2,
+        in_specs=[pl.BlockSpec(memory_space=pl.ANY)] * 4,
         out_specs=(vmem,) * 5,
         scratch_shapes=[
             pltpu.VMEM((tokens, width), bf16),
             pltpu.VMEM((nout * ncol, rows, ta), bf16),
             pltpu.VMEM(activations.shape, bf16),
             pltpu.VMEM((nout, rows, ta), bf16),
+            pltpu.VMEM((rows,), f32),
+            pltpu.VMEM((width,), f32),
             pltpu.VMEM((rows, 128), f32),
             pltpu.VMEM((nout, 1, width), f32),
             pltpu.VMEM((nz, 1, width), f32),
@@ -394,7 +406,7 @@
             dma((nout * ncol,)),
             dma((nout,)),
             dma((nout, ncol)),
-            dma((3,)),
+            dma((5,)),
             dma((nout,)), dma((nout,)),
             dma((nz,)), dma((nz,)),
             dma((ncol,)), dma((ncol,)),

time: 115 us -> 111 us (0.965)
  Pallas kernels: 112 us -> 109 us
    pallas_call x1, Pallas kernels: 109 us -> 106 us  [body(): pl.pallas_call(functools.partial(kernel, nout, nz, ncol, 1.0 / tokens **...]
where the time goes in v5:
time: 111 us
  Pallas kernels  109 us (98%)
  local copies, waits for them, and re-layouts  1.4 us (1%)
    pallas_call x1, Pallas kernels, body(): pl.pallas_call(functools.partial(kernel, nout, nz, ncol, 1.0 / tokens **...  106 us
    pallas_call x1, Pallas kernels, body(): pl.pallas_call(functools.partial(update_kernel, step), grid=(parts,), out...  3.18 us

profile of v5, /device:TPU:0, one launch (start us, length us, event | category | flops | bytes accessed | tf_op | source)
XLA Modules:
  0.0 111.0 jit_solution(3029757928029688957)
XLA Ops:
  0.6 0.0 copy-start
  0.6 0.7 copy-done
  1.3 0.0 copy-start.1
  1.4 0.7 copy-done.1
  2.0 105.8 %shard_map.67 = (f32[576,4096]{1,0:T(8,128)S(1)}, f32[1,576]{1,0:T(1,128)S(1)}, f32[576,128]{1,0:T(8,128)S(1)}, f32[1,4096]{1,0:T(1,128)S(1)}, f32[1,128]{1,0:T(1,128)S(1)}) custom-call(bf16[256,2304]{1,0:T(8,128)(2,1)} %raw_ref.1, bf16[128,4096]{1,0:T(8,128)(2,1)} %g_ref.1, f32[576]{0:T(1024)S(1)} %copy-done.1, f32[4096]{0:T(1024)S(1)} %copy-done), custom_call_target="tpu_custom_call" | custom-call | tf_op jit(solution)/shard_map/pallas_call | solution.py:377
  107.8 3.2 %shard_map.68 = (bf16[576,4096]{1,0:T(8,128)(2,1)}, f32[576]{0:T(1024)}, f32[4096]{0:T(1024)}) custom-call(f32[576,4096]{1,0:T(8,128)S(1)} %get-tuple-element.8.grad_ref, f32[576,128]{1,0:T(8,128)S(1)} %get-tuple-element.9.nr_ref, f32[1,4096]{1,0:T(1,128)S(1)} %get-tuple-element.10.nc_ref, f32[1,128]{1,0:T(1,128)S(1)} %get-tuple-element.11.mt_ref, ...), custom_call_target="tpu_custom_call" | custom-call | tf_op jit(solution)/shard_map/pallas_call | solution.py:422
Async XLA Ops:
  0.6 0.7 copy-start
  1.3 0.7 copy-start.1

commit v6 on v5

--- a/solution.py
+++ b/solution.py
@@ -11,8 +11,8 @@
 F = 8192
 STEP = 2
 MESH = pl.DeviceIdType.MESH
-PIECES = 4
-BY_Y = 1
+PIECES = 8
+BY_Y = 2
 
 
 def kernel(
@@ -175,7 +175,7 @@
 
                 to_partner(here, o, z + s, h).start()
 
-            if s == 1 and h == 0:
+            if s == 1 and h == 1:
                 for d in range(1, nout):
                     a_first(d).start()
                 for d in range(1, ncol):

time: 111 us -> 111 us (level)
  no operation moved by 1% of the time
where the time goes in v6:
time: 111 us
  Pallas kernels  109 us (98%)
  local copies, waits for them, and re-layouts  1.4 us (1%)
    pallas_call x1, Pallas kernels, body(): pl.pallas_call(functools.partial(kernel, nout, nz, ncol, 1.0 / tokens **...  106 us
    pallas_call x1, Pallas kernels, body(): pl.pallas_call(functools.partial(update_kernel, step), grid=(parts,), out...  3.18 us

profile of v6, /device:TPU:0, one launch (start us, length us, event | category | flops | bytes accessed | tf_op | source)
XLA Modules:
  0.0 111.2 jit_solution(10822732825376044272)
XLA Ops:
  0.6 0.0 copy-start
  0.6 0.7 copy-done
  1.3 0.0 copy-start.1
  1.4 0.7 copy-done.1
  2.0 106.0 %shard_map.67 = (f32[576,4096]{1,0:T(8,128)S(1)}, f32[1,576]{1,0:T(1,128)S(1)}, f32[576,128]{1,0:T(8,128)S(1)}, f32[1,4096]{1,0:T(1,128)S(1)}, f32[1,128]{1,0:T(1,128)S(1)}) custom-call(bf16[256,2304]{1,0:T(8,128)(2,1)} %raw_ref.1, bf16[128,4096]{1,0:T(8,128)(2,1)} %g_ref.1, f32[576]{0:T(1024)S(1)} %copy-done.1, f32[4096]{0:T(1024)S(1)} %copy-done), custom_call_target="tpu_custom_call" | custom-call | tf_op jit(solution)/shard_map/pallas_call | solution.py:377
  108.0 3.2 %shard_map.68 = (bf16[576,4096]{1,0:T(8,128)(2,1)}, f32[576]{0:T(1024)}, f32[4096]{0:T(1024)}) custom-call(f32[576,4096]{1,0:T(8,128)S(1)} %get-tuple-element.8.grad_ref, f32[576,128]{1,0:T(8,128)S(1)} %get-tuple-element.9.nr_ref, f32[1,4096]{1,0:T(1,128)S(1)} %get-tuple-element.10.nc_ref, f32[1,128]{1,0:T(1,128)S(1)} %get-tuple-element.11.mt_ref, ...), custom_call_target="tpu_custom_call" | custom-call | tf_op jit(solution)/shard_map/pallas_call | solution.py:422
Async XLA Ops:
  0.6 0.7 copy-start
  1.3 0.7 copy-start.1
